TPU v7x, 32 devices: a whole 2x2x4 slice. The times are simulated.
32 devices in a mesh: strip: 4 (over y, core), depth: 8 (over z, x).
Axes of the slice: x: 2, y: 2, z: 4, core: 2. Of those that a mesh axis runs over, the one named last changes fastest.
Arguments:
- position: float32 [4, 8, 3, 32, 128], P('strip', 'depth'), may hold values from -2.4 to 2.4
- velocity: float32 [4, 8, 3, 32, 128], P('strip', 'depth'), may hold values from -3 to 3
- stress: float32 [4, 8, 6, 32, 128], P('strip', 'depth'), may hold values from -6 to 6
- plastic: float32 [4, 8, 32, 128], P('strip', 'depth'), may hold values from 0.005 to 0.2
- particle_mass: float32 [4, 8, 32, 128], P('strip', 'depth'), may hold values from 0.004 to 0.016
- density: float32 [4, 8, 32, 128], P('strip', 'depth'), may hold values from 0.6 to 1.6
- cohesion: float32 [4, 8, 32, 128], P('strip', 'depth'), may hold values from 0.3 to 1.2
- counts: int32 [4, 8, 32], P('strip', 'depth'), may hold values from 32 to 128, as said below
- block_pairs: int32 [4, 8, 128, 2], P('strip', 'depth'), may hold values from 0 to 31, as said below
- pair_count: int32 [4, 8], P('strip', 'depth'), may hold values from 32 to 128, as said below
- send_lists: int32 [4, 8, 4, 16], P('strip', 'depth'), may hold values from 0 to 31, as said below
- cross_links: int32 [4, 8, 2, 48, 2], P('strip', 'depth'), may hold values from 0 to 15, as said below
- contact: int32 [4, 8, 16], P('strip', 'depth'), may hold values from 0 to 32, as said below
Outputs:
- new_position: float32 [4, 8, 3, 32, 128], P('strip', 'depth')
- new_velocity: float32 [4, 8, 3, 32, 128], P('strip', 'depth')
- new_stress: float32 [4, 8, 6, 32, 128], P('strip', 'depth')
- new_plastic: float32 [4, 8, 32, 128], P('strip', 'depth')
Inputs may be any that keep to these rules, and one draw needn't show every extreme that they name: A block's live particles are its first counts slots; every device has a full block. `pair_count`: at least 32; some device reaches 128. `block_pairs`: the first pair_count entries of a device hold each of its blocks paired with itself once and distinct unordered pairs of different blocks, each at most once, in either order; later entries are to be ignored. `send_lists`: each face lists 16 distinct blocks; faces 0, 1 look to the next and previous device along depth, 2, 3 along strip. `cross_links`: entry (f, q) = (a, b): slot a of the device's list 2f meets slot b of the next device's list 2f + 1; a face's entries are distinct. `contact`: 32 stands for no block; a device's entries are either all 32 or 16 distinct blocks.
All inputs are finite; a program needn't handle non-finite values.
Results may differ from a plain program's by a relative error of at most 0.0003.
Values sent between devices are 32-bit elements; how exact they have to be, the bound alone decides.
A program may use at most 64 MiB of HBM per device.

v0:
```python
import jax
import jax.numpy as jnp
from jax import lax
from jax.sharding import PartitionSpec as P

RETURN_ITERS = 4


smooth_len = 1.5
kernel_coef = -105.0 / (3.141592653589793 * 1.5**5)
time_step = 0.25
gravity = 1.0
spin_rate = 2.0
blade_stiff = 4.0
bulk_mod = 2.0
shear_mod = 1.5
friction = 0.25
harden_scale = 0.05
harden_mod = 0.5
relax_rate = 0.7
tau_floor = 0.5
group_tiles = 32
voigt_index = ((0, 3, 5), (3, 1, 4), (5, 4, 2))
voigt_pairs = ((0, 0), (1, 1), (2, 2), (0, 1), (1, 2), (0, 2))


def from_behind(block, axis, distance):
    devices = range(lax.axis_size(axis))
    route = [(i - distance, i) for i in devices if i - distance in devices]
    return lax.ppermute(block, axis, route)


def passed_along(value, axis, steps):
    count = lax.axis_size(axis)
    pairs = [(source, (source + steps) % count) for source in range(count)]
    return lax.ppermute(value, axis, pairs)


def source_rows(places, motion, stress, particle_mass, density, occupied):
    safe_density = jnp.where(occupied > 0.0, density, 1.0)
    weighted_mass = particle_mass * occupied
    volume = weighted_mass / safe_density
    scaled = stress / (safe_density * safe_density)[..., None, :]
    feature_rows = [weighted_mass]
    for row_axis in range(3):
        feature_rows.append(weighted_mass * places[..., row_axis, :])
    for component in range(6):
        feature_rows.append(weighted_mass * scaled[..., component, :])
    for row_axis in range(3):
        dotted = scaled[..., voigt_index[row_axis][0], :] * places[..., 0, :]
        dotted = dotted + scaled[..., voigt_index[row_axis][1], :] * places[..., 1, :]
        dotted = dotted + scaled[..., voigt_index[row_axis][2], :] * places[..., 2, :]
        feature_rows.append(weighted_mass * dotted)
    feature_rows.append(volume)
    for row_axis in range(3):
        feature_rows.append(volume * motion[..., row_axis, :])
    for row_axis in range(3):
        feature_rows.append(volume * places[..., row_axis, :])
    for row_axis, col_axis in voigt_pairs:
        paired = (
            motion[..., row_axis, :] * places[..., col_axis, :]
            + motion[..., col_axis, :] * places[..., row_axis, :]
        )
        feature_rows.append(volume * (0.5 * paired))
    return jnp.stack(feature_rows, axis=-2)


def pair_kernel(row_places, col_places, weight):
    squared = jnp.zeros(
        row_places.shape[:-2] + (row_places.shape[-1], col_places.shape[-1]), jnp.float32
    )
    for row_axis in range(3):
        spread = row_places[..., row_axis, :, None] - col_places[..., row_axis, None, :]
        squared = squared + spread * spread
    closeness = jnp.maximum(1.0 - jnp.sqrt(squared) / smooth_len, 0.0)
    return kernel_coef * closeness * closeness * closeness * weight[..., None, None]


def tile_sums(row_sources, row_places, col_sources, col_places, links_in, tile_total, halve_self):
    length = links_in.shape[0]
    padded = -(-length // group_tiles) * group_tiles
    links_padded = jnp.pad(links_in, ((0, padded - length), (0, 0)))
    offsets = jnp.arange(group_tiles, dtype=jnp.int32)

    def one_group(group_index, carried):
        row_summed, col_summed = carried
        portion = lax.dynamic_slice_in_dim(links_padded, group_index * group_tiles, group_tiles, 0)
        row_block = portion[:, 0]
        col_block = portion[:, 1]
        weight = jnp.where(group_index * group_tiles + offsets < tile_total, 1.0, 0.0).astype(
            jnp.float32
        )
        if halve_self:
            weight = weight * jnp.where(row_block == col_block, 0.5, 1.0)
        kernel = pair_kernel(row_places[row_block], col_places[col_block], weight)
        to_rows = jnp.einsum(
            "tkj,tij->tki", col_sources[col_block], kernel, precision=lax.Precision.HIGHEST
        )
        row_summed = row_summed.at[row_block].add(to_rows)
        to_cols = jnp.einsum(
            "tki,tij->tkj", row_sources[row_block], kernel, precision=lax.Precision.HIGHEST
        )
        col_summed = col_summed.at[col_block].add(to_cols)
        return (row_summed, col_summed)

    groups = (tile_total + group_tiles - 1) // group_tiles
    start_sums = (
        jnp.zeros(row_sources.shape, jnp.float32),
        jnp.zeros(col_sources.shape, jnp.float32),
    )
    return lax.fori_loop(0, groups, one_group, start_sums)


def section_rates(summed, places, motion, stress, density, contact_flag):
    scaled = stress / (density * density)[..., None, :]
    blade_motion = (
        spin_rate * places[..., 2, :],
        jnp.zeros_like(places[..., 1, :]),
        -spin_rate * places[..., 0, :],
    )
    acceleration = []
    for row_axis in range(3):
        total_force = jnp.zeros_like(summed[..., 0, :])
        for col_axis in range(3):
            voigt_slot = voigt_index[row_axis][col_axis]
            total_force = total_force + scaled[..., voigt_slot, :] * (
                places[..., col_axis, :] * summed[..., 0, :] - summed[..., 1 + col_axis, :]
            )
            total_force = total_force + places[..., col_axis, :] * summed[..., 4 + voigt_slot, :]
        total_force = total_force - summed[..., 10 + row_axis, :]
        total_force = total_force + blade_stiff * contact_flag * (
            blade_motion[row_axis] - motion[..., row_axis, :]
        )
        if row_axis == 2:
            total_force = total_force - gravity
        acceleration.append(total_force)
    strain = []
    for component, (row_axis, col_axis) in enumerate(voigt_pairs):
        strain_rate = 0.5 * (
            places[..., col_axis, :] * summed[..., 14 + row_axis, :]
            + places[..., row_axis, :] * summed[..., 14 + col_axis, :]
        )
        strain_rate = strain_rate - summed[..., 20 + component, :]
        strain_rate = strain_rate - 0.5 * summed[..., 13, :] * (
            motion[..., row_axis, :] * places[..., col_axis, :]
            + motion[..., col_axis, :] * places[..., row_axis, :]
        )
        strain_rate = strain_rate + 0.5 * (
            motion[..., row_axis, :] * summed[..., 17 + col_axis, :]
            + motion[..., col_axis, :] * summed[..., 17 + row_axis, :]
        )
        strain.append(strain_rate)
    return (jnp.stack(acceleration, axis=-2), jnp.stack(strain, axis=-2))


def elastic_step(stress, strain, fraction):
    volumetric = strain[..., 0, :] + strain[..., 1, :] + strain[..., 2, :]
    lame_first = bulk_mod - 2.0 * shear_mod / 3.0
    components = []
    for component in range(6):
        change = 2.0 * shear_mod * strain[..., component, :]
        if component < 3:
            change = change + lame_first * volumetric
        components.append(stress[..., component, :] + fraction * time_step * change)
    return components


def plastic_return(components, plastic, cohesion):
    for iteration in range(RETURN_ITERS):
        mean_stress = (components[0] + components[1] + components[2]) / 3.0
        deviator = [
            components[0] - mean_stress,
            components[1] - mean_stress,
            components[2] - mean_stress,
            components[3],
            components[4],
            components[5],
        ]
        second = 0.5 * (
            deviator[0] * deviator[0] + deviator[1] * deviator[1] + deviator[2] * deviator[2]
        )
        second = (
            second
            + deviator[3] * deviator[3]
            + deviator[4] * deviator[4]
            + deviator[5] * deviator[5]
        )
        shear_norm = jnp.sqrt(second)
        yield_limit = cohesion * (1.0 + plastic / (plastic + harden_scale))
        excess = jnp.maximum(shear_norm + friction * 3.0 * mean_stress - yield_limit, 0.0)
        multiplier = (
            relax_rate * excess / (shear_mod + 9.0 * bulk_mod * friction * friction + harden_mod)
        )
        shrink = jnp.maximum(1.0 - shear_mod * multiplier / jnp.maximum(shear_norm, tau_floor), 0.0)
        mean_stress = mean_stress - 3.0 * bulk_mod * friction * multiplier
        components = [
            deviator[0] * shrink + mean_stress,
            deviator[1] * shrink + mean_stress,
            deviator[2] * shrink + mean_stress,
            deviator[3] * shrink,
            deviator[4] * shrink,
            deviator[5] * shrink,
        ]
        plastic = plastic + multiplier
    return (jnp.stack(components, axis=-2), plastic)


def fetch_depth(values_in, offset):
    return from_behind(values_in, "depth", offset)


def fetch_strip(values_in, offset):
    return passed_along(values_in, "strip", offset)


def hand_back_depth(values_in):
    return from_behind(values_in, "depth", 1)


def hand_back_strip(values_in):
    return passed_along(values_in, "strip", 1)


def shards(
    position,
    velocity,
    stress,
    plastic,
    particle_mass,
    density,
    cohesion,
    counts,
    block_pairs,
    pair_count,
    send_lists,
    cross_links,
    contact,
):
    places = jnp.swapaxes(position[0, 0], 0, 1)
    motion = jnp.swapaxes(velocity[0, 0], 0, 1)
    stress_blocks = jnp.swapaxes(stress[0, 0], 0, 1)
    plastic_now = plastic[0, 0]
    mass_now = particle_mass[0, 0]
    density_now = density[0, 0]
    cohesion_now = cohesion[0, 0]
    pairs_now = block_pairs[0, 0]
    pair_total = pair_count[0, 0]
    rim_lists = send_lists[0, 0]
    links_now = cross_links[0, 0]
    blocks = places.shape[0]
    occupied = (
        jnp.arange(places.shape[-1], dtype=jnp.int32)[None, :] < counts[0, 0][:, None]
    ).astype(jnp.float32)
    contact_flag = jnp.sum(
        (contact[0, 0][:, None] == jnp.arange(blocks, dtype=jnp.int32)[None, :]).astype(
            jnp.float32
        ),
        axis=0,
    )[:, None]

    def interact(cur_places, cur_motion, cur_stress):
        sources = source_rows(cur_places, cur_motion, cur_stress, mass_now, density_now, occupied)
        row_part, col_part = tile_sums(
            sources, cur_places, sources, cur_places, pairs_now, pair_total, True
        )
        summed = row_part + col_part
        for face_index in range(2):
            up_rim = rim_lists[2 * face_index]
            down_rim = rim_lists[2 * face_index + 1]
            face_links = links_now[face_index]
            fetch_rows = fetch_depth if face_index == 0 else fetch_strip
            hand_back = hand_back_depth if face_index == 0 else hand_back_strip
            received = fetch_rows(
                jnp.concatenate([cur_places[down_rim], sources[down_rim]], axis=1), -1
            )
            far_sources = received[:, 3:]
            far_places = received[:, 0:3]
            own_part, far_part = tile_sums(
                sources[up_rim],
                cur_places[up_rim],
                far_sources,
                far_places,
                face_links,
                face_links.shape[0],
                False,
            )
            summed = summed.at[up_rim].add(own_part)
            summed = summed.at[down_rim].add(hand_back(far_part))
        return summed

    summed = interact(places, motion, stress_blocks)
    acceleration, strain = section_rates(
        summed, places, motion, stress_blocks, density_now, contact_flag
    )
    half_motion = motion + 0.5 * time_step * acceleration
    half_places = places + 0.5 * time_step * motion
    half_stress = plastic_return(
        elastic_step(stress_blocks, strain, 0.5), plastic_now, cohesion_now
    )[0]
    summed = interact(half_places, half_motion, half_stress)
    acceleration, strain = section_rates(
        summed, half_places, half_motion, half_stress, density_now, contact_flag
    )
    new_motion = motion + time_step * acceleration
    new_places = places + time_step * half_motion
    new_stress, new_plastic = plastic_return(
        elastic_step(stress_blocks, strain, 1.0), plastic_now, cohesion_now
    )
    particle_keep = occupied[:, None, :]
    new_position = jnp.swapaxes(new_places * particle_keep, 0, 1)[None, None]
    new_velocity = jnp.swapaxes(new_motion * particle_keep, 0, 1)[None, None]
    new_stress_out = jnp.swapaxes(new_stress * particle_keep, 0, 1)[None, None]
    new_plastic_out = (new_plastic * occupied)[None, None]
    return (new_position, new_velocity, new_stress_out, new_plastic_out)


def solution(mesh):
    return jax.shard_map(
        shards,
        mesh=mesh,
        in_specs=(
            P("strip", "depth", None, None, None),
            P("strip", "depth", None, None, None),
            P("strip", "depth", None, None, None),
            P("strip", "depth", None, None),
            P("strip", "depth", None, None),
            P("strip", "depth", None, None),
            P("strip", "depth", None, None),
            P("strip", "depth", None),
            P("strip", "depth", None, None),
            P("strip", "depth"),
            P("strip", "depth", None, None),
            P("strip", "depth", None, None, None),
            P("strip", "depth", None),
        ),
        out_specs=(
            P("strip", "depth", None, None, None),
            P("strip", "depth", None, None, None),
            P("strip", "depth", None, None, None),
            P("strip", "depth", None, None),
        ),
        check_vma=False,
    )
```

profile of v0, /device:TPU:28, one launch (start us, length us, event | category | flops | bytes accessed | tf_op | source)
XLA Modules:
  0.0 353.0 jit_solution(8684530957393822783)
XLA Ops:
  13.4 71.8 %while.90 = (s32[]{:T(128)}, f32[32,26,128]{2,1,0:T(8,128)S(1)}, f32[32,26,128]{2,1,0:T(8,128)S(1)}, s32[]{:T(128)}, s32[128,2]{0,1:T(2,128)S(1)}, /*index=5*/f3...) while((s32[]{:T(128)}, f32[32,26,128]{2,1,0:T(8,128)S(1)}, ...), condition=%wide.region_3.4_spmd.clone, body=%wide.region_0.3_spmd.clone.sunk | while | flops 343099776 | bytes 6564663 | solution.py:111
  16.1 6.1 %fusion.457 = f32[32,26,128]{2,1,0:T(8,128)S(1)} fusion(f32[32,26,128]{2,1,0:T(8,128)S(1)} %gather_fusion, f32[32]{0:T(128)S(1)} %fusion.454, f32[32,128]{1,0:T(8,128)S(1)} %bitcast.559, f32[32,128]{1,0:T(8,128)S(1)} %bitcast.595, f32[32,128]{1,0:T(8,128)S(1)} %bitcast.557, f32[32,128]{1,0:T(8,128)S(1)} %bitcast.593, f32[32,128]{1,0:T(8,128)S(1)} %bitcast.555, ...), kind=kOutput, calls=%fused_computation.69.clone.1 | convolution fusion | flops 171442176 | bytes 950400 | tf_op jit(solution)/shard_map/while/body/tkj,tij->tki/dot_general | solution.py:96
  34.0 6.1 %fusion.457 = f32[32,26,128]{2,1,0:T(8,128)S(1)} fusion(f32[32,26,128]{2,1,0:T(8,128)S(1)} %gather_fusion, f32[32]{0:T(128)S(1)} %fusion.454, f32[32,128]{1,0:T(8,128)S(1)} %bitcast.559, f32[32,128]{1,0:T(8,128)S(1)} %bitcast.595, f32[32,128]{1,0:T(8,128)S(1)} %bitcast.557, f32[32,128]{1,0:T(8,128)S(1)} %bitcast.593, f32[32,128]{1,0:T(8,128)S(1)} %bitcast.555, ...), kind=kOutput, calls=%fused_computation.69.clone.1 | convolution fusion | flops 171442176 | bytes 950400 | tf_op jit(solution)/shard_map/while/body/tkj,tij->tki/dot_general | solution.py:96
  42.5 4.9 %fusion.458 = f32[32,26,128]{2,1,0:T(8,128)S(1)} fusion(f32[32,26,128]{2,1,0:T(8,128)S(1)} %gather_fusion.3, f32[32]{0:T(128)S(1)} %fusion.454, f32[32,128]{1,0:T(8,128)S(1)} %bitcast.560, f32[32,128]{1,0:T(8,128)S(1)} %bitcast.596, f32[32,128]{1,0:T(8,128)S(1)} %bitcast.558, f32[32,128]{1,0:T(8,128)S(1)} %bitcast.594, f32[32,128]{1,0:T(8,128)S(1)} %bitcast.556, ...), kind=kOutput, calls=%fused_computation.68.clone.1 | convolution fusion | flops 171442176 | bytes 950400 | tf_op jit(solution)/shard_map/while/body/tki,tij->tkj/dot_general | solution.py:100
  52.0 6.1 %fusion.457 = f32[32,26,128]{2,1,0:T(8,128)S(1)} fusion(f32[32,26,128]{2,1,0:T(8,128)S(1)} %gather_fusion, f32[32]{0:T(128)S(1)} %fusion.454, f32[32,128]{1,0:T(8,128)S(1)} %bitcast.559, f32[32,128]{1,0:T(8,128)S(1)} %bitcast.595, f32[32,128]{1,0:T(8,128)S(1)} %bitcast.557, f32[32,128]{1,0:T(8,128)S(1)} %bitcast.593, f32[32,128]{1,0:T(8,128)S(1)} %bitcast.555, ...), kind=kOutput, calls=%fused_computation.69.clone.1 | convolution fusion | flops 171442176 | bytes 950400 | tf_op jit(solution)/shard_map/while/body/tkj,tij->tki/dot_general | solution.py:96
  60.5 4.9 %fusion.458 = f32[32,26,128]{2,1,0:T(8,128)S(1)} fusion(f32[32,26,128]{2,1,0:T(8,128)S(1)} %gather_fusion.3, f32[32]{0:T(128)S(1)} %fusion.454, f32[32,128]{1,0:T(8,128)S(1)} %bitcast.560, f32[32,128]{1,0:T(8,128)S(1)} %bitcast.596, f32[32,128]{1,0:T(8,128)S(1)} %bitcast.558, f32[32,128]{1,0:T(8,128)S(1)} %bitcast.594, f32[32,128]{1,0:T(8,128)S(1)} %bitcast.556, ...), kind=kOutput, calls=%fused_computation.68.clone.1 | convolution fusion | flops 171442176 | bytes 950400 | tf_op jit(solution)/shard_map/while/body/tki,tij->tkj/dot_general | solution.py:100
  69.9 6.1 %fusion.457 = f32[32,26,128]{2,1,0:T(8,128)S(1)} fusion(f32[32,26,128]{2,1,0:T(8,128)S(1)} %gather_fusion, f32[32]{0:T(128)S(1)} %fusion.454, f32[32,128]{1,0:T(8,128)S(1)} %bitcast.559, f32[32,128]{1,0:T(8,128)S(1)} %bitcast.595, f32[32,128]{1,0:T(8,128)S(1)} %bitcast.557, f32[32,128]{1,0:T(8,128)S(1)} %bitcast.593, f32[32,128]{1,0:T(8,128)S(1)} %bitcast.555, ...), kind=kOutput, calls=%fused_computation.69.clone.1 | convolution fusion | flops 171442176 | bytes 950400 | tf_op jit(solution)/shard_map/while/body/tkj,tij->tki/dot_general | solution.py:96
  78.4 4.9 %fusion.458 = f32[32,26,128]{2,1,0:T(8,128)S(1)} fusion(f32[32,26,128]{2,1,0:T(8,128)S(1)} %gather_fusion.3, f32[32]{0:T(128)S(1)} %fusion.454, f32[32,128]{1,0:T(8,128)S(1)} %bitcast.560, f32[32,128]{1,0:T(8,128)S(1)} %bitcast.596, f32[32,128]{1,0:T(8,128)S(1)} %bitcast.558, f32[32,128]{1,0:T(8,128)S(1)} %bitcast.594, f32[32,128]{1,0:T(8,128)S(1)} %bitcast.556, ...), kind=kOutput, calls=%fused_computation.68.clone.1 | convolution fusion | flops 171442176 | bytes 950400 | tf_op jit(solution)/shard_map/while/body/tki,tij->tkj/dot_general | solution.py:100
  88.0 34.7 %while.91 = (s32[]{:T(128)}, f32[16,26,128]{2,1,0:T(8,128)S(1)}, f32[16,26,128]{2,1,0:T(8,128)S(1)}, s32[64,2]{0,1:T(2,128)S(1)}, f32[16,26,128]{2,1,0:T(8,128)S...) while((s32[]{:T(128)}, f32[16,26,128]{2,1,0:T(8,128)S(1)}, ...), condition=%wide.region_7.8_spmd.clone, body=%wide.region_4.7_spmd.clone.sunk | while | flops 343099680 | bytes 6564403 | solution.py:111
  90.0 6.1 %fusion.466 = f32[32,26,128]{2,1,0:T(8,128)S(1)} fusion(f32[32,26,128]{2,1,0:T(8,128)S(1)} %gather_fusion.4, f32[32]{0:T(128)S(1)} %compare_select_fusion.28, f32[32,128]{1,0:T(8,128)S(1)} %bitcast.565, f32[32,128]{1,0:T(8,128)S(1)} %bitcast.601, f32[32,128]{1,0:T(8,128)S(1)} %bitcast.563, f32[32,128]{1,0:T(8,128)S(1)} %bitcast.599, ...), kind=kOutput, calls=%fused_computation.115.clone.1 | convolution fusion | flops 171442176 | bytes 950400 | tf_op jit(solution)/shard_map/while/body/eval_jaxpr/tkj,tij->tki/dot_general | solution.py:96
  107.3 6.1 %fusion.466 = f32[32,26,128]{2,1,0:T(8,128)S(1)} fusion(f32[32,26,128]{2,1,0:T(8,128)S(1)} %gather_fusion.4, f32[32]{0:T(128)S(1)} %compare_select_fusion.28, f32[32,128]{1,0:T(8,128)S(1)} %bitcast.565, f32[32,128]{1,0:T(8,128)S(1)} %bitcast.601, f32[32,128]{1,0:T(8,128)S(1)} %bitcast.563, f32[32,128]{1,0:T(8,128)S(1)} %bitcast.599, ...), kind=kOutput, calls=%fused_computation.115.clone.1 | convolution fusion | flops 171442176 | bytes 950400 | tf_op jit(solution)/shard_map/while/body/eval_jaxpr/tkj,tij->tki/dot_general | solution.py:96
  126.5 34.7 %while.92 = (s32[]{:T(128)}, f32[16,26,128]{2,1,0:T(8,128)S(1)}, f32[16,26,128]{2,1,0:T(8,128)S(1)}, s32[64,2]{0,1:T(2,128)S(1)}, f32[16,26,128]{2,1,0:T(8,128)S...) while((s32[]{:T(128)}, f32[16,26,128]{2,1,0:T(8,128)S(1)}, ...), condition=%wide.region_13.14_spmd.clone, body=%wide.region_10.13_spmd.clone.sunk | while | flops 343099680 | bytes 6564403 | solution.py:111
  128.5 6.1 %fusion.475 = f32[32,26,128]{2,1,0:T(8,128)S(1)} fusion(f32[32,26,128]{2,1,0:T(8,128)S(1)} %gather_fusion.8, f32[32]{0:T(128)S(1)} %compare_select_fusion.29, f32[32,128]{1,0:T(8,128)S(1)} %bitcast.571, f32[32,128]{1,0:T(8,128)S(1)} %bitcast.607, f32[32,128]{1,0:T(8,128)S(1)} %bitcast.569, f32[32,128]{1,0:T(8,128)S(1)} %bitcast.605, ...), kind=kOutput, calls=%fused_computation.158.clone.1 | convolution fusion | flops 171442176 | bytes 950400 | tf_op jit(solution)/shard_map/while/body/eval_jaxpr/tkj,tij->tki/dot_general | solution.py:96
  145.8 6.1 %fusion.475 = f32[32,26,128]{2,1,0:T(8,128)S(1)} fusion(f32[32,26,128]{2,1,0:T(8,128)S(1)} %gather_fusion.8, f32[32]{0:T(128)S(1)} %compare_select_fusion.29, f32[32,128]{1,0:T(8,128)S(1)} %bitcast.571, f32[32,128]{1,0:T(8,128)S(1)} %bitcast.607, f32[32,128]{1,0:T(8,128)S(1)} %bitcast.569, f32[32,128]{1,0:T(8,128)S(1)} %bitcast.605, ...), kind=kOutput, calls=%fused_computation.158.clone.1 | convolution fusion | flops 171442176 | bytes 950400 | tf_op jit(solution)/shard_map/while/body/eval_jaxpr/tkj,tij->tki/dot_general | solution.py:96
  154.4 4.9 %fusion.476 = f32[32,26,128]{2,1,0:T(8,128)S(1)} fusion(f32[32,26,128]{2,1,0:T(8,128)S(1)} %gather_fusion.11, f32[32]{0:T(128)S(1)} %compare_select_fusion.29, f32[32,128]{1,0:T(8,128)S(1)} %bitcast.572, f32[32,128]{1,0:T(8,128)S(1)} %bitcast.608, f32[32,128]{1,0:T(8,128)S(1)} %bitcast.570, f32[32,128]{1,0:T(8,128)S(1)} %bitcast.606, ...), kind=kOutput, calls=%fused_computation.157.clone.1 | convolution fusion | flops 171442176 | bytes 950400 | tf_op jit(solution)/shard_map/while/body/eval_jaxpr/tki,tij->tkj/dot_general | solution.py:100
  183.7 34.7 %while.94 = (s32[]{:T(128)}, f32[16,26,128]{2,1,0:T(8,128)S(1)}, f32[16,26,128]{2,1,0:T(8,128)S(1)}, s32[64,2]{0,1:T(2,128)S(1)}, f32[16,26,128]{2,1,0:T(8,128)S...) while((s32[]{:T(128)}, f32[16,26,128]{2,1,0:T(8,128)S(1)}, ...), condition=%wide.region_24.25_spmd.clone, body=%wide.region_21.24_spmd.clone.sunk | while | flops 343099680 | bytes 6564403 | solution.py:111
  185.7 6.1 %fusion.494 = f32[32,26,128]{2,1,0:T(8,128)S(1)} fusion(f32[32,26,128]{2,1,0:T(8,128)S(1)} %gather_fusion.16, f32[32]{0:T(128)S(1)} %compare_select_fusion.30, f32[32,128]{1,0:T(8,128)S(1)} %bitcast.577, f32[32,128]{1,0:T(8,128)S(1)} %bitcast.613, f32[32,128]{1,0:T(8,128)S(1)} %bitcast.575, f32[32,128]{1,0:T(8,128)S(1)} %bitcast.611, ...), kind=kOutput, calls=%fused_computation.247.clone.1 | convolution fusion | flops 171442176 | bytes 950400 | tf_op jit(solution)/shard_map/while/body/eval_jaxpr/tkj,tij->tki/dot_general | solution.py:96
  203.0 6.1 %fusion.494 = f32[32,26,128]{2,1,0:T(8,128)S(1)} fusion(f32[32,26,128]{2,1,0:T(8,128)S(1)} %gather_fusion.16, f32[32]{0:T(128)S(1)} %compare_select_fusion.30, f32[32,128]{1,0:T(8,128)S(1)} %bitcast.577, f32[32,128]{1,0:T(8,128)S(1)} %bitcast.613, f32[32,128]{1,0:T(8,128)S(1)} %bitcast.575, f32[32,128]{1,0:T(8,128)S(1)} %bitcast.611, ...), kind=kOutput, calls=%fused_computation.247.clone.1 | convolution fusion | flops 171442176 | bytes 950400 | tf_op jit(solution)/shard_map/while/body/eval_jaxpr/tkj,tij->tki/dot_general | solution.py:96
  222.2 40.5 %while.95 = (s32[]{:T(128)}, f32[16,26,128]{2,1,0:T(8,128)S(1)}, f32[16,26,128]{2,1,0:T(8,128)S(1)}, s32[64,2]{0,1:T(2,128)S(1)}, f32[16,26,128]{2,1,0:T(8,128)S...) while((s32[]{:T(128)}, f32[16,26,128]{2,1,0:T(8,128)S(1)}, ...), condition=%wide.region_30.31_spmd.clone, body=%wide.region_27.30_spmd.clone.sunk | while | flops 343099680 | bytes 6630507 | solution.py:111
  225.3 6.7 %fusion.503 = f32[32,26,128]{2,1,0:T(8,128)S(1)} fusion(f32[32,26,128]{2,1,0:T(8,128)S(1)} %gather_fusion.20, f32[32]{0:T(128)} %compare_select_fusion.31, f32[32,128]{1,0:T(8,128)S(1)} %bitcast.583, f32[32,128]{1,0:T(8,128)S(1)} %bitcast.619, f32[32,128]{1,0:T(8,128)S(1)} %bitcast.581, f32[32,128]{1,0:T(8,128)S(1)} %bitcast.617, ...), kind=kOutput, calls=%fused_computation.290.clone.1 | convolution fusion | flops 171442176 | bytes 950400 | tf_op jit(solution)/shard_map/while/body/eval_jaxpr/tkj,tij->tki/dot_general | solution.py:96
  234.6 5.9 %fusion.504 = f32[32,26,128]{2,1,0:T(8,128)S(1)} fusion(f32[32,26,128]{2,1,0:T(8,128)S(1)} %gather_fusion.23, f32[32]{0:T(128)} %compare_select_fusion.31, f32[32,128]{1,0:T(8,128)S(1)} %bitcast.584, f32[32,128]{1,0:T(8,128)} %bitcast.620, f32[32,128]{1,0:T(8,128)S(1)} %bitcast.582, f32[32,128]{1,0:T(8,128)S(1)} %bitcast.618, ...), kind=kOutput, calls=%fused_computation.289.clone.1 | convolution fusion | flops 171442176 | bytes 950400 | tf_op jit(solution)/shard_map/while/body/eval_jaxpr/tki,tij->tkj/dot_general | solution.py:100
  245.6 6.7 %fusion.503 = f32[32,26,128]{2,1,0:T(8,128)S(1)} fusion(f32[32,26,128]{2,1,0:T(8,128)S(1)} %gather_fusion.20, f32[32]{0:T(128)} %compare_select_fusion.31, f32[32,128]{1,0:T(8,128)S(1)} %bitcast.583, f32[32,128]{1,0:T(8,128)S(1)} %bitcast.619, f32[32,128]{1,0:T(8,128)S(1)} %bitcast.581, f32[32,128]{1,0:T(8,128)S(1)} %bitcast.617, ...), kind=kOutput, calls=%fused_computation.290.clone.1 | convolution fusion | flops 171442176 | bytes 950400 | tf_op jit(solution)/shard_map/while/body/eval_jaxpr/tkj,tij->tki/dot_general | solution.py:96
  254.8 5.9 %fusion.504 = f32[32,26,128]{2,1,0:T(8,128)S(1)} fusion(f32[32,26,128]{2,1,0:T(8,128)S(1)} %gather_fusion.23, f32[32]{0:T(128)} %compare_select_fusion.31, f32[32,128]{1,0:T(8,128)S(1)} %bitcast.584, f32[32,128]{1,0:T(8,128)} %bitcast.620, f32[32,128]{1,0:T(8,128)S(1)} %bitcast.582, f32[32,128]{1,0:T(8,128)S(1)} %bitcast.618, ...), kind=kOutput, calls=%fused_computation.289.clone.1 | convolution fusion | flops 171442176 | bytes 950400 | tf_op jit(solution)/shard_map/while/body/eval_jaxpr/tki,tij->tkj/dot_general | solution.py:100
  263.3 78.6 %while.93 = (s32[]{:T(128)}, f32[32,26,128]{2,1,0:T(8,128)S(1)}, f32[32,26,128]{2,1,0:T(8,128)S(1)}, s32[]{:T(128)}, s32[128,2]{0,1:T(2,128)S(1)}, /*index=5*/f3...) while((s32[]{:T(128)}, f32[32,26,128]{2,1,0:T(8,128)S(1)}, ...), condition=%wide.region_20.21_spmd.clone, body=%wide.region_17.20_spmd.clone.sunk | while | flops 343099776 | bytes 6564663 | solution.py:111
  266.8 6.1 %fusion.485 = f32[32,26,128]{2,1,0:T(8,128)S(1)} fusion(f32[32,26,128]{2,1,0:T(8,128)} %gather_fusion.12, f32[32]{0:T(128)S(1)} %fusion.482, f32[32,128]{1,0:T(8,128)S(1)} %bitcast.589, f32[32,128]{1,0:T(8,128)S(1)} %bitcast.625, f32[32,128]{1,0:T(8,128)S(1)} %bitcast.587, f32[32,128]{1,0:T(8,128)S(1)} %bitcast.623, f32[32,128]{1,0:T(8,128)S(1)} %bitcast.585, ...), kind=kOutput, calls=%fused_computation.201.clone.1 | convolution fusion | flops 171442176 | bytes 950400 | tf_op jit(solution)/shard_map/while/body/tkj,tij->tki/dot_general | solution.py:96
  276.2 4.9 %fusion.486 = f32[32,26,128]{2,1,0:T(8,128)S(1)} fusion(f32[32,26,128]{2,1,0:T(8,128)} %gather_fusion.15, f32[32]{0:T(128)S(1)} %fusion.482, f32[32,128]{1,0:T(8,128)S(1)} %bitcast.590, f32[32,128]{1,0:T(8,128)S(1)} %bitcast.626, f32[32,128]{1,0:T(8,128)S(1)} %bitcast.588, f32[32,128]{1,0:T(8,128)S(1)} %bitcast.624, f32[32,128]{1,0:T(8,128)S(1)} %bitcast.586, ...), kind=kOutput, calls=%fused_computation.200.clone.1 | convolution fusion | flops 171442176 | bytes 950400 | tf_op jit(solution)/shard_map/while/body/tki,tij->tkj/dot_general | solution.py:100
  286.4 6.1 %fusion.485 = f32[32,26,128]{2,1,0:T(8,128)S(1)} fusion(f32[32,26,128]{2,1,0:T(8,128)} %gather_fusion.12, f32[32]{0:T(128)S(1)} %fusion.482, f32[32,128]{1,0:T(8,128)S(1)} %bitcast.589, f32[32,128]{1,0:T(8,128)S(1)} %bitcast.625, f32[32,128]{1,0:T(8,128)S(1)} %bitcast.587, f32[32,128]{1,0:T(8,128)S(1)} %bitcast.623, f32[32,128]{1,0:T(8,128)S(1)} %bitcast.585, ...), kind=kOutput, calls=%fused_computation.201.clone.1 | convolution fusion | flops 171442176 | bytes 950400 | tf_op jit(solution)/shard_map/while/body/tkj,tij->tki/dot_general | solution.py:96
  295.8 4.9 %fusion.486 = f32[32,26,128]{2,1,0:T(8,128)S(1)} fusion(f32[32,26,128]{2,1,0:T(8,128)} %gather_fusion.15, f32[32]{0:T(128)S(1)} %fusion.482, f32[32,128]{1,0:T(8,128)S(1)} %bitcast.590, f32[32,128]{1,0:T(8,128)S(1)} %bitcast.626, f32[32,128]{1,0:T(8,128)S(1)} %bitcast.588, f32[32,128]{1,0:T(8,128)S(1)} %bitcast.624, f32[32,128]{1,0:T(8,128)S(1)} %bitcast.586, ...), kind=kOutput, calls=%fused_computation.200.clone.1 | convolution fusion | flops 171442176 | bytes 950400 | tf_op jit(solution)/shard_map/while/body/tki,tij->tkj/dot_general | solution.py:100
  306.1 6.1 %fusion.485 = f32[32,26,128]{2,1,0:T(8,128)S(1)} fusion(f32[32,26,128]{2,1,0:T(8,128)} %gather_fusion.12, f32[32]{0:T(128)S(1)} %fusion.482, f32[32,128]{1,0:T(8,128)S(1)} %bitcast.589, f32[32,128]{1,0:T(8,128)S(1)} %bitcast.625, f32[32,128]{1,0:T(8,128)S(1)} %bitcast.587, f32[32,128]{1,0:T(8,128)S(1)} %bitcast.623, f32[32,128]{1,0:T(8,128)S(1)} %bitcast.585, ...), kind=kOutput, calls=%fused_computation.201.clone.1 | convolution fusion | flops 171442176 | bytes 950400 | tf_op jit(solution)/shard_map/while/body/tkj,tij->tki/dot_general | solution.py:96
  315.5 4.9 %fusion.486 = f32[32,26,128]{2,1,0:T(8,128)S(1)} fusion(f32[32,26,128]{2,1,0:T(8,128)} %gather_fusion.15, f32[32]{0:T(128)S(1)} %fusion.482, f32[32,128]{1,0:T(8,128)S(1)} %bitcast.590, f32[32,128]{1,0:T(8,128)S(1)} %bitcast.626, f32[32,128]{1,0:T(8,128)S(1)} %bitcast.588, f32[32,128]{1,0:T(8,128)S(1)} %bitcast.624, f32[32,128]{1,0:T(8,128)S(1)} %bitcast.586, ...), kind=kOutput, calls=%fused_computation.200.clone.1 | convolution fusion | flops 171442176 | bytes 950400 | tf_op jit(solution)/shard_map/while/body/tki,tij->tkj/dot_general | solution.py:100
  325.8 6.1 %fusion.485 = f32[32,26,128]{2,1,0:T(8,128)S(1)} fusion(f32[32,26,128]{2,1,0:T(8,128)} %gather_fusion.12, f32[32]{0:T(128)S(1)} %fusion.482, f32[32,128]{1,0:T(8,128)S(1)} %bitcast.589, f32[32,128]{1,0:T(8,128)S(1)} %bitcast.625, f32[32,128]{1,0:T(8,128)S(1)} %bitcast.587, f32[32,128]{1,0:T(8,128)S(1)} %bitcast.623, f32[32,128]{1,0:T(8,128)S(1)} %bitcast.585, ...), kind=kOutput, calls=%fused_computation.201.clone.1 | convolution fusion | flops 171442176 | bytes 950400 | tf_op jit(solution)/shard_map/while/body/tkj,tij->tki/dot_general | solution.py:96
  335.1 4.9 %fusion.486 = f32[32,26,128]{2,1,0:T(8,128)S(1)} fusion(f32[32,26,128]{2,1,0:T(8,128)} %gather_fusion.15, f32[32]{0:T(128)S(1)} %fusion.482, f32[32,128]{1,0:T(8,128)S(1)} %bitcast.590, f32[32,128]{1,0:T(8,128)S(1)} %bitcast.626, f32[32,128]{1,0:T(8,128)S(1)} %bitcast.588, f32[32,128]{1,0:T(8,128)S(1)} %bitcast.624, f32[32,128]{1,0:T(8,128)S(1)} %bitcast.586, ...), kind=kOutput, calls=%fused_computation.200.clone.1 | convolution fusion | flops 171442176 | bytes 950400 | tf_op jit(solution)/shard_map/while/body/tki,tij->tkj/dot_general | solution.py:100
  (434 shorter events, 199.5 us)
Async XLA Ops:
  0.6 1.7 copy-start.11
  0.6 1.7 copy-start
  0.7 1.6 copy-start.1
  1.5 1.1 copy-start.18
  1.5 1.1 copy-start.4
  2.6 1.4 copy-start.2
  4.9 157.3 %copy-start.27 = (s32[16]{0:T(128)}, s32[16]{0:T(128)S(1)}, u32[]{:S(2)}) copy-start(s32[16]{0:T(128)S(1)} %get-tuple-element.1222) | copy-start | bytes 196
  4.9 158.5 %copy-start.25 = (s32[16]{0:T(128)}, s32[16]{0:T(128)S(1)}, u32[]{:S(2)}) copy-start(s32[16]{0:T(128)S(1)} %get-tuple-element.1221) | copy-start | bytes 196
  5.0 160.5 %copy-start.23 = (s32[16]{0:T(128)}, s32[16]{0:T(128)S(1)}, u32[]{:S(2)}) copy-start(s32[16]{0:T(128)S(1)} %get-tuple-element.1223) | copy-start | bytes 196
  5.0 162.2 %copy-start.21 = (s32[16]{0:T(128)}, s32[16]{0:T(128)S(1)}, u32[]{:S(2)}) copy-start(s32[16]{0:T(128)S(1)} %get-tuple-element.1220) | copy-start | bytes 196
  6.9 81.0 %collective-permute-start = (f32[16,29,128]{2,1,0:T(8,128)}, f32[16,29,128]{2,1,0:T(8,128)S(1)}, u32[]{:S(2)}, u32[]{:S(2)}) collective-permute-start(f32[16,29,128]{2,1,0:T(8,128)} %pad_maximum_fusion), channel_id=1, source_target_pairs={{1,0},{2,1},{3,2},{4,3},{5,4},{6,5},{7,6},{9,8},{10,9},{11,10},{12... | collective-permute-start | bytes 712712 | tf_op jit(solution)/shard_map/ppermute | solution.py:30
  12.0 112.5 %collective-permute-start.2 = (f32[16,29,128]{2,1,0:T(8,128)}, f32[16,29,128]{2,1,0:T(8,128)}, u32[]{:S(2)}, u32[]{:S(2)}) collective-permute-start(f32[16,29,128]{2,1,0:T(8,128)} %pad_maximum_fusion.1), channel_id=1, source_target_pairs={{0,24},{8,0},{16,8},{24,16},{1,25},{9,1},{17,9},{25,17},{2,26},{10... | collective-permute-start | bytes 712712 | tf_op jit(solution)/shard_map/ppermute | solution.py:36
  13.4 71.8 %copy-start.30 = (s32[1,1,2,48,2]{3,4,2,1,0:T(2,128)S(1)}, s32[1,1,2,48,2]{3,4,2,1,0:T(2,128)}, u32[]{:S(2)}) copy-start(s32[1,1,2,48,2]{3,4,2,1,0:T(2,128)} %param.36) | copy-start | bytes 2308
  13.4 71.8 %copy-start.31 = (s32[1,1,16]{2,1,0:T(1,128)S(1)}, s32[1,1,16]{2,1,0:T(1,128)}, u32[]{:S(2)}) copy-start(s32[1,1,16]{2,1,0:T(1,128)} %param.37) | copy-start | bytes 196
  87.9 81.7 %copy-start.13 = (f32[32,128]{1,0:T(8,128)}, f32[32,128]{1,0:T(8,128)S(1)}, u32[]{:S(2)}) copy-start(f32[32,128]{1,0:T(8,128)S(1)} %fusion.351) | copy-start | bytes 49156
  122.6 40.8 %collective-permute-start.1 = (f32[16,26,128]{2,1,0:T(8,128)S(1)}, f32[16,26,128]{2,1,0:T(8,128)}, u32[]{:S(2)}, u32[]{:S(2)}) collective-permute-start(f32[16,26,128]{2,1,0:T(8,128)S(1)} %get-tuple-element.725), channel_id=1, source_target_pairs={{0,1},{1,2},{2,3},{3,4},{4,5},{5,6},{6,7},{8,9},{9,10},{10,11},{11... | collective-permute-start | bytes 638984 | tf_op jit(solution)/shard_map/ppermute | solution.py:30
  161.1 6.0 %collective-permute-start.3 = (f32[16,26,128]{2,1,0:T(8,128)S(1)}, f32[16,26,128]{2,1,0:T(8,128)S(1)}, u32[]{:S(2)}, u32[]{:S(2)}) collective-permute-start(f32[16,26,128]{2,1,0:T(8,128)S(1)} %get-tuple-element.727), channel_id=1, source_target_pairs={{0,8},{8,16},{16,24},{24,0},{1,9},{9,17},{17,25},{25,1},{2,10},{10... | collective-permute-start | bytes 638984 | tf_op jit(solution)/shard_map/ppermute | solution.py:36
  162.2 7.2 %copy-start.19 = (f32[32]{0:T(128)}, f32[32]{0:T(128)S(1)}, u32[]{:S(2)}) copy-start(f32[32]{0:T(128)S(1)} %broadcast_multiply_fusion) | copy-start | bytes 388
  169.3 1.2 copy-start.5
  169.5 1.1 copy-start.7
  169.5 1.1 copy-start.8
  174.0 9.6 %collective-permute-start.4 = (f32[16,29,128]{2,1,0:T(8,128)S(1)}, f32[16,29,128]{2,1,0:T(8,128)S(1)}, u32[]{:S(2)}, u32[]{:S(2)}) collective-permute-start(f32[16,29,128]{2,1,0:T(8,128)S(1)} %pad_maximum_fusion.2), channel_id=1, source_target_pairs={{1,0},{2,1},{3,2},{4,3},{5,4},{6,5},{7,6},{9,8},{10,9},{11,10},{12... | collective-permute-start | bytes 712712 | tf_op jit(solution)/shard_map/ppermute | solution.py:30
  183.0 37.3 %collective-permute-start.6 = (f32[16,29,128]{2,1,0:T(8,128)}, f32[16,29,128]{2,1,0:T(8,128)}, u32[]{:S(2)}, u32[]{:S(2)}) collective-permute-start(f32[16,29,128]{2,1,0:T(8,128)} %pad_maximum_fusion.3), channel_id=1, source_target_pairs={{0,24},{8,0},{16,8},{24,16},{1,25},{9,1},{17,9},{25,17},{2,26},{10... | collective-permute-start | bytes 712712 | tf_op jit(solution)/shard_map/ppermute | solution.py:36
  218.4 125.5 %collective-permute-start.5 = (f32[16,26,128]{2,1,0:T(8,128)S(1)}, f32[16,26,128]{2,1,0:T(8,128)}, u32[]{:S(2)}, u32[]{:S(2)}) collective-permute-start(f32[16,26,128]{2,1,0:T(8,128)S(1)} %get-tuple-element.731), channel_id=1, source_target_pairs={{0,1},{1,2},{2,3},{3,4},{4,5},{5,6},{6,7},{8,9},{9,10},{10,11},{11... | collective-permute-start | bytes 638984 | tf_op jit(solution)/shard_map/ppermute | solution.py:30
  222.3 1.1 copy-start.15
  242.5 1.1 copy-start.15
  262.7 84.3 %collective-permute-start.7 = (f32[16,26,128]{2,1,0:T(8,128)S(1)}, f32[16,26,128]{2,1,0:T(8,128)}, u32[]{:S(2)}, u32[]{:S(2)}) collective-permute-start(f32[16,26,128]{2,1,0:T(8,128)S(1)} %get-tuple-element.733), channel_id=1, source_target_pairs={{0,8},{8,16},{16,24},{24,0},{1,9},{9,17},{17,25},{25,1},{2,10},{10... | collective-permute-start | bytes 638984 | tf_op jit(solution)/shard_map/ppermute | solution.py:36
  342.1 1.8 copy-start.26
  343.8 2.0 copy-start.24
  345.8 1.2 copy-start.22
  350.8 1.3 copy-start.9
  350.8 1.3 copy-start.20
  (10 other events, 7.4 us)
where the time goes:
time: 357 us; the launch traced here: 353 us
  matrix products  179 us (50%)
  other arithmetic  88.6 us (25%)
  local copies, waits for them, and re-layouts  67.2 us (19%)
  starting transfers between devices  13.1 us (4%)
    dot_general x16, matrix products, one_group(): jnp.einsum('tkj,tij->tki', col_sources[col_block], kernel, precision=lax....  98.5 us
    dot_general x16, matrix products, one_group(): jnp.einsum('tki,tij->tkj', row_sources[row_block], kernel, precision=lax....  80.6 us
    scatter-add x16, other arithmetic, one_group(): row_summed = row_summed.at[row_block].add(to_rows)  29.9 us
    scatter-add x16, other arithmetic, one_group(): col_summed = col_summed.at[col_block].add(to_cols)  29.7 us
    gather x32, local copies, waits for them, and re-layouts, one_group(): kernel = pair_kernel(row_places[row_block], col_places[col_block], weight)  19.5 us
    gather x16, local copies, waits for them, and re-layouts, one_group(): row_sources[row_block]  12.6 us
    gather x16, local copies, waits for them, and re-layouts, one_group(): col_sources[col_block]  12.6 us
    ppermute x4, starting transfers between devices, from_behind(): return lax.ppermute(block, axis, route)  11.9 us
  transfers between devices with their start and end apart: 8, of which 2 were waited for; matrix products, arithmetic and copies ran while one was open for 89% of the time, Pallas kernels for 0%

commit v1 on v0

v1 whole, which is shorter than its diff:
```python
import functools

import jax
import jax.numpy as jnp
from jax import lax
from jax.experimental import pallas as pl
from jax.experimental.pallas import tpu as pltpu
from jax.sharding import PartitionSpec as P

RETURN_ITERS = 4

smooth_len = 1.5
kernel_coef = -105.0 / (3.141592653589793 * 1.5**5)
time_step = 0.25
gravity = 1.0
spin_rate = 2.0
blade_stiff = 4.0
bulk_mod = 2.0
shear_mod = 1.5
friction = 0.25
harden_scale = 0.05
harden_mod = 0.5
relax_rate = 0.7
tau_floor = 0.5
voigt_index = ((0, 3, 5), (3, 1, 4), (5, 4, 2))
voigt_pairs = ((0, 0), (1, 1), (2, 2), (0, 1), (1, 2), (0, 2))

STATE = 16
SOURCES = 26
ROWS = 32
FEATURES = 32
UNROLL = 4
f32 = jnp.float32
bf16 = jnp.bfloat16


def from_behind(block, axis, distance):
    devices = range(lax.axis_size(axis))
    route = [(i - distance, i) for i in devices if i - distance in devices]
    return lax.ppermute(block, axis, route)


def passed_along(value, axis, steps):
    count = lax.axis_size(axis)
    pairs = [(source, (source + steps) % count) for source in range(count)]
    return lax.ppermute(value, axis, pairs)


def source_rows(x, v, s, mass, volume):
    rows = [mass]
    rows += [mass * x[k] for k in range(3)]
    rows += [mass * s[c] for c in range(6)]
    for k in range(3):
        i = voigt_index[k]
        rows.append(mass * (s[i[0]] * x[0] + s[i[1]] * x[1] + s[i[2]] * x[2]))
    rows.append(volume)
    rows += [volume * v[k] for k in range(3)]
    rows += [volume * x[k] for k in range(3)]
    for a, b in voigt_pairs:
        rows.append(volume * (0.5 * (v[a] * x[b] + v[b] * x[a])))
    return rows


def split3(value):
    high = value.astype(bf16).astype(f32)
    rest = value - high
    mid = rest.astype(bf16).astype(f32)
    low = (rest - mid).astype(bf16).astype(f32)
    return high, mid, low


PRODUCTS = ((0, 0), (0, 1), (1, 0), (1, 1), (0, 2), (2, 0))


def distance_rows(x, row_side, col_side):
    scaled = [x[k] * (1.0 / smooth_len) for k in range(3)]
    parts = [split3(y) for y in scaled]
    norm = split3(scaled[0] * scaled[0] + scaled[1] * scaled[1] + scaled[2] * scaled[2])
    one = jnp.ones_like(x[0])
    zero = jnp.zeros_like(x[0])
    left, right = [], []
    for k in range(3):
        for a, b in PRODUCTS:
            left.append(-2.0 * parts[k][a])
            right.append(parts[k][b])
    left += list(norm) + [one] * 3
    right += [one] * 3 + list(norm)
    fill = FEATURES - len(left)
    return (left + [zero] * fill if row_side else None, right + [zero] * fill if col_side else None)


def put_rows(ref, rows, start, count, stride):
    for k, row in enumerate(rows):
        ref[pl.ds(start * stride + k, count, stride=stride), :] = row


def get_row(ref, k, count, stride):
    return ref[pl.ds(k, count, stride=stride), :]


def close_kernel(left, right, weight):
    squared = lax.dot_general(left, right, (((1,), (0,)), ((), ())), preferred_element_type=f32)
    squared = jnp.maximum(squared, 1e-30)
    near = jnp.maximum(1.0 - squared * lax.rsqrt(squared), 0.0)
    cubed = near * near * (near if weight is None else near * weight)
    return cubed.astype(bf16)


def fold(result):
    return result[:ROWS] + result[ROWS:]


def to_rows(sources, kernel):
    return fold(
        lax.dot_general(sources, kernel, (((1,), (1,)), ((), ())), preferred_element_type=f32)
    )


def to_cols(sources, kernel):
    return fold(
        lax.dot_general(sources, kernel, (((1,), (0,)), ((), ())), preferred_element_type=f32)
    )


def store_sources(tmp, src, start, count):
    def one(b, carry):
        rows = tmp[pl.ds(pl.multiple_of(b * ROWS, ROWS), ROWS), :]
        high = rows.astype(bf16)
        src[start + b, 0:ROWS, :] = high
        src[start + b, ROWS : 2 * ROWS, :] = (rows - high.astype(f32)).astype(bf16)
        return carry

    lax.fori_loop(0, count, one, 0, unroll=4)


def store_cols(tmp, col, start, count):
    def one(b, carry):
        col[start + b] = tmp[pl.ds(pl.multiple_of(b * FEATURES, FEATURES), FEATURES), :].astype(bf16)
        return carry

    lax.fori_loop(0, count, one, 0, unroll=4)


def gather_rims(rows, raw, lists, sends, blocks):
    put_rows(raw, rows, 0, blocks, STATE)
    for face in range(4):
        for slot in range(lists.shape[1]):
            at = pl.multiple_of(lists[face, slot] * STATE, STATE)
            sends[face][slot * STATE : (slot + 1) * STATE, :] = raw[pl.ds(at, STATE), :]


def begin_kernel(
    counts, lists, pos, vel, stress, mass, density, state, s0, s1, s2, s3, occ, raw
):
    blocks, parts = mass.shape
    lane = lax.broadcasted_iota(jnp.int32, (1, parts), 1)
    for b in range(blocks):
        occ[b : b + 1, :] = jnp.where(lane < counts[b], 1.0, 0.0)
    live = occ[...]
    rho = density[...]
    inverse = 1.0 / (rho * rho)
    weighted = mass[...] * live * kernel_coef
    rows = [pos[k] for k in range(3)] + [vel[k] for k in range(3)]
    rows += [stress[c] * inverse for c in range(6)]
    rows += [weighted, weighted / rho, live, inverse]
    for k, row in enumerate(rows):
        state[k] = row
    gather_rims(rows, raw, lists, (s0, s1, s2, s3), blocks)


def local_kernel(pairs, total, state, acc, left, tmp, src, right):
    blocks = state.shape[1]
    x = [state[k] for k in range(3)]
    v = [state[k] for k in range(3, 6)]
    s = [state[k] for k in range(6, 12)]
    zero = jnp.zeros_like(x[0])
    rows = source_rows(x, v, s, state[12], state[13])
    put_rows(tmp, rows + [zero] * (ROWS - SOURCES), 0, blocks, ROWS)
    store_sources(tmp, src, 0, blocks)
    left_rows, right_rows = distance_rows(x, True, True)
    put_rows(tmp, right_rows, 0, blocks, FEATURES)
    store_cols(tmp, right, 0, blocks)
    put_rows(tmp, left_rows, 0, blocks, FEATURES)

    def turn(b, carry):
        block = tmp[pl.ds(pl.multiple_of(b * FEATURES, FEATURES), FEATURES), :]
        left[b] = block.T.astype(bf16)
        acc[b] = jnp.zeros(acc.shape[1:], f32)
        return carry

    lax.fori_loop(0, blocks, turn, 0, unroll=4)
    live = total[0, 0]
    last = pairs.shape[0] - 1

    def group(g, carry):
        found = []
        for u in range(UNROLL):
            q = g * UNROLL + u
            at = jnp.minimum(q, last)
            a, b = pairs[at, 0], pairs[at, 1]
            a = jnp.where(q < live, a, 0)
            b = jnp.where(q < live, b, 0)
            weight = jnp.where(q < live, jnp.where(a == b, 0.5, 1.0), 0.0)
            kernel = close_kernel(left[a], right[b], weight)
            found.append((a, to_rows(src[b], kernel)))
            found.append((b, to_cols(src[a], kernel)))
        for at, value in found:
            acc[at] += value
        return carry

    lax.fori_loop(0, (live + UNROLL - 1) // UNROLL, group, 0)


def cross_sums(lists, links, links_behind, far, acc_in, left, acc, tmp, src, right):
    rim = lists.shape[1]
    for f in range(4):
        got = [get_row(far[f], k, rim, STATE) for k in range(14)]
        zero = jnp.zeros_like(got[0])
        rows = source_rows(got[0:3], got[3:6], got[6:12], got[12], got[13])
        put_rows(tmp, rows + [zero] * (ROWS - SOURCES), f * rim, rim, ROWS)
    store_sources(tmp, src, 0, 4 * rim)
    for f in range(4):
        got = [get_row(far[f], k, rim, STATE) for k in range(3)]
        put_rows(tmp, distance_rows(got, False, True)[1], f * rim, rim, FEATURES)
    store_cols(tmp, right, 0, 4 * rim)
    acc[...] = acc_in[...]

    def group(q, carry):
        found = []
        for face in range(2):
            own = lists[2 * face, links[face, q, 0]]
            slot = 2 * face * rim + links[face, q, 1]
            found.append((own, to_rows(src[slot], close_kernel(left[own], right[slot], None))))
            own = lists[2 * face + 1, links_behind[face][q, 1]]
            slot = (2 * face + 1) * rim + links_behind[face][q, 0]
            found.append((own, to_rows(src[slot], close_kernel(left[own], right[slot], None))))
        for at, value in found:
            acc[at] += value
        return carry

    lax.fori_loop(0, links.shape[1], group, 0)


def section_rates(summed, x, v, s, contact_flag):
    blade = (spin_rate * x[2], jnp.zeros_like(x[1]), -spin_rate * x[0])
    acceleration = []
    arm = [x[l] * summed[0] - summed[1 + l] for l in range(3)]
    for k in range(3):
        total = -summed[10 + k] + blade_stiff * contact_flag * (blade[k] - v[k])
        for l in range(3):
            slot = voigt_index[k][l]
            total = total + s[slot] * arm[l] + x[l] * summed[4 + slot]
        if k == 2:
            total = total - gravity
        acceleration.append(total)
    strain = []
    for c, (k, l) in enumerate(voigt_pairs):
        rate = 0.5 * (x[l] * summed[14 + k] + x[k] * summed[14 + l]) - summed[20 + c]
        rate = rate - 0.5 * summed[13] * (v[k] * x[l] + v[l] * x[k])
        rate = rate + 0.5 * (v[k] * summed[17 + l] + v[l] * summed[17 + k])
        strain.append(rate)
    return acceleration, strain


def elastic_step(stress, strain, fraction):
    volumetric = strain[0] + strain[1] + strain[2]
    lame_first = bulk_mod - 2.0 * shear_mod / 3.0
    components = []
    for c in range(6):
        change = 2.0 * shear_mod * strain[c]
        if c < 3:
            change = change + lame_first * volumetric
        components.append(stress[c] + fraction * time_step * change)
    return components


def plastic_return(c, plastic, cohesion):
    for _ in range(RETURN_ITERS):
        mean = (c[0] + c[1] + c[2]) / 3.0
        d = [c[0] - mean, c[1] - mean, c[2] - mean, c[3], c[4], c[5]]
        second = 0.5 * (d[0] * d[0] + d[1] * d[1] + d[2] * d[2])
        second = second + d[3] * d[3] + d[4] * d[4] + d[5] * d[5]
        tau = jnp.sqrt(second)
        limit = cohesion * (1.0 + plastic / (plastic + harden_scale))
        excess = jnp.maximum(tau + friction * 3.0 * mean - limit, 0.0)
        multiplier = (
            relax_rate * excess / (shear_mod + 9.0 * bulk_mod * friction * friction + harden_mod)
        )
        shrink = jnp.maximum(1.0 - shear_mod * multiplier / jnp.maximum(tau, tau_floor), 0.0)
        mean = mean - 3.0 * bulk_mod * friction * multiplier
        c = [
            d[0] * shrink + mean,
            d[1] * shrink + mean,
            d[2] * shrink + mean,
            d[3] * shrink,
            d[4] * shrink,
            d[5] * shrink,
        ]
        plastic = plastic + multiplier
    return c, plastic


def contact_rows(contact, flag, blocks):
    flag[...] = jnp.zeros_like(flag)
    for i in range(contact.shape[0]):
        flag[pl.ds(contact[i], 1), :] += 1.0
    return flag[0:blocks, :]


def rates_of(acc, state, contact, flag):
    blocks, parts = state.shape[1:]
    contact_flag = contact_rows(contact, flag, blocks)
    x = [state[k] for k in range(3)]
    v = [state[k] for k in range(3, 6)]
    s = [state[k] for k in range(6, 12)]
    summed = [acc[:, k, :] for k in range(SOURCES)]
    return x, v, *section_rates(summed, x, v, s, contact_flag)


def half_kernel(
    lists, links, behind_depth, behind_strip, contact,
    acc_in, left, d_next, d_prev, s_next, s_prev, state, stress, plastic, cohesion,
    state_out, s0, s1, s2, s3,
    acc, tmp, src, right, flag, raw,
):
    blocks = state.shape[1]
    cross_sums(
        lists, links, (behind_depth, behind_strip), (d_next, d_prev, s_next, s_prev),
        acc_in, left, acc, tmp, src, right,
    )
    x, v, acceleration, strain = rates_of(acc, state, contact, flag)
    components, _ = plastic_return(
        elastic_step([stress[c] for c in range(6)], strain, 0.5), plastic[...], cohesion[...]
    )
    inverse = state[15]
    rows = [x[k] + 0.5 * time_step * v[k] for k in range(3)]
    rows += [v[k] + 0.5 * time_step * acceleration[k] for k in range(3)]
    rows += [c * inverse for c in components]
    rows += [state[12], state[13], state[14], inverse]
    for k, row in enumerate(rows):
        state_out[k] = row
    gather_rims(rows, raw, lists, (s0, s1, s2, s3), blocks)


def end_kernel(
    lists, links, behind_depth, behind_strip, contact,
    acc_in, left, d_next, d_prev, s_next, s_prev, state, stress, plastic, cohesion, position, velocity,
    new_position, new_velocity, new_stress, new_plastic,
    acc, tmp, src, right, flag,
):
    cross_sums(
        lists, links, (behind_depth, behind_strip), (d_next, d_prev, s_next, s_prev),
        acc_in, left, acc, tmp, src, right,
    )
    _, half_v, acceleration, strain = rates_of(acc, state, contact, flag)
    components, hardened = plastic_return(
        elastic_step([stress[c] for c in range(6)], strain, 1.0), plastic[...], cohesion[...]
    )
    live = state[14]
    for k in range(3):
        new_position[k] = (position[k] + time_step * half_v[k]) * live
        new_velocity[k] = (velocity[k] + time_step * acceleration[k]) * live
    for c in range(6):
        new_stress[c] = components[c] * live
    new_plastic[...] = hardened * live


def shards(
    position, velocity, stress, plastic, particle_mass, density, cohesion,
    counts, block_pairs, pair_count, send_lists, cross_links, contact,
):
    position, velocity, stress = position[0, 0], velocity[0, 0], stress[0, 0]
    plastic, mass, density, cohesion = plastic[0, 0], particle_mass[0, 0], density[0, 0], cohesion[0, 0]
    counts, pairs, lists = counts[0, 0], block_pairs[0, 0], send_lists[0, 0]
    links, contact = cross_links[0, 0], contact[0, 0]
    blocks, parts = mass.shape
    rim = lists.shape[1]
    smem = pl.BlockSpec(memory_space=pltpu.SMEM)
    vmem = pl.BlockSpec(memory_space=pltpu.VMEM)
    shape = jax.ShapeDtypeStruct
    state_shape = shape((STATE, blocks, parts), f32)
    send_shape = shape((rim * STATE, parts), f32)
    acc_shape = shape((blocks, ROWS, parts), f32)
    left_shape = shape((blocks, parts, FEATURES), bf16)
    far_scratch = [
        pltpu.VMEM((blocks, ROWS, parts), f32),
        pltpu.VMEM((4 * rim * ROWS, parts), f32),
        pltpu.VMEM((4 * rim, 2 * ROWS, parts), bf16),
        pltpu.VMEM((4 * rim, FEATURES, parts), bf16),
        pltpu.VMEM((blocks + 8, parts), f32),
    ]
    raw_scratch = pltpu.VMEM((blocks * STATE, parts), f32)
    params = pltpu.CompilerParams(vmem_limit_bytes=24 << 20)

    behind_depth = from_behind(links[0], "depth", 1)
    behind_strip = passed_along(links[1], "strip", 1)

    def exchange(sends):
        return (
            from_behind(sends[1], "depth", -1),
            from_behind(sends[0], "depth", 1),
            passed_along(sends[3], "strip", -1),
            passed_along(sends[2], "strip", 1),
        )

    def local(state):
        tiles = pairs.shape[0]
        return pl.pallas_call(
            local_kernel,
            out_shape=(acc_shape, left_shape),
            in_specs=[smem, smem, vmem],
            out_specs=(vmem, vmem),
            scratch_shapes=[
                pltpu.VMEM((blocks * ROWS, parts), f32),
                pltpu.VMEM((blocks, 2 * ROWS, parts), bf16),
                pltpu.VMEM((blocks, FEATURES, parts), bf16),
            ],
            compiler_params=params,
            cost_estimate=pl.CostEstimate(
                flops=tiles * parts * parts * 600, bytes_accessed=8 << 20, transcendentals=0
            ),
            name="local_tiles",
        )(pairs, pair_count, state)

    state, *sends = pl.pallas_call(
        begin_kernel,
        out_shape=(state_shape,) + (send_shape,) * 4,
        in_specs=[smem] * 2 + [vmem] * 5,
        out_specs=(vmem,) * 5,
        scratch_shapes=[pltpu.VMEM((blocks, parts), f32), raw_scratch],
        compiler_params=params,
        name="begin",
    )(counts, lists, position, velocity, stress, mass, density)
    far = exchange(sends)
    acc, left = local(state)
    half, *sends = pl.pallas_call(
        half_kernel,
        out_shape=(state_shape,) + (send_shape,) * 4,
        in_specs=[smem] * 5 + [vmem] * 10,
        out_specs=(vmem,) * 5,
        scratch_shapes=far_scratch + [raw_scratch],
        compiler_params=params,
        name="half_step",
    )(
        lists, links, behind_depth, behind_strip, contact,
        acc, left, *far, state, stress, plastic, cohesion,
    )
    far = exchange(sends)
    acc, left = local(half)
    outs = pl.pallas_call(
        end_kernel,
        out_shape=(
            shape(position.shape, f32),
            shape(velocity.shape, f32),
            shape(stress.shape, f32),
            shape(plastic.shape, f32),
        ),
        in_specs=[smem] * 5 + [vmem] * 12,
        out_specs=(vmem,) * 4,
        scratch_shapes=far_scratch,
        compiler_params=params,
        name="full_step",
    )(
        lists, links, behind_depth, behind_strip, contact,
        acc, left, *far, half, stress, plastic, cohesion, position, velocity,
    )
    return tuple(out[None, None] for out in outs)


def solution(mesh):
    def spec(rank):
        return P("strip", "depth", *([None] * (rank - 2)))

    return jax.shard_map(
        shards,
        mesh=mesh,
        in_specs=tuple(spec(r) for r in (5, 5, 5, 4, 4, 4, 4, 3, 4, 2, 4, 5, 3)),
        out_specs=tuple(spec(r) for r in (5, 5, 5, 4)),
        check_vma=False,
    )
```

time: 357 us -> 145 us (0.41)
  the two profiles are of different devices: /device:TPU:28 before, /device:TPU:6 now
where the time goes in v1:
time: 145 us; the launch traced here: 143 us
  Pallas kernels  116 us (80%)
  starting transfers between devices  17.1 us (12%)
  local copies, waits for them, and re-layouts  6.26 us (4%)
  waiting for transfers between devices  1.77 us (1%)
  between operations  1.52 us (1%)
    pallas_call x2, Pallas kernels, local(): pl.pallas_call(local_kernel, out_shape=(acc_shape, left_shape), in_specs=...  57.7 us
    pallas_call x1, Pallas kernels, shards(): pl.pallas_call(end_kernel, out_shape=(shape(position.shape, f32), shape(v...  29.2 us
    pallas_call x1, Pallas kernels, shards(): pl.pallas_call(half_kernel, out_shape=(state_shape,) + (send_shape,) * 4,...  28.5 us
    ppermute x5, starting transfers between devices, from_behind(): return lax.ppermute(block, axis, route)  16 us
    unnamed x32, local copies, waits for them, and re-layouts  6.07 us
  transfers between devices with their start and end apart: 10, of which 1 were waited for; matrix products, arithmetic and copies ran while one was open for 0% of the time, Pallas kernels for 40%

profile of v1, /device:TPU:6, one launch (start us, length us, event | category | flops | bytes accessed | tf_op | source)
XLA Modules:
  0.0 142.9 jit_solution(6749828765168186223)
XLA Ops:
  0.7 0.7 copy-done.8
  1.3 0.9 copy-done
  2.2 0.8 copy-done.2
  3.0 0.8 copy-done.4
  3.8 0.7 copy-done.9
  4.5 0.7 copy-done.10
  5.2 0.7 begin.1
  6.0 2.4 %collective-permute-start.2 = (f32[256,128]{1,0:T(8,128)S(1)}, f32[256,128]{1,0:T(8,128)S(1)}, u32[]{:S(2)}, u32[]{:S(2)}) collective-permute-start(f32[256,128]{1,0:T(8,128)S(1)} %get-tuple-element.25), channel_id=1, source_target_pairs={{1,0},{2,1},{3,2},{4,3},{5,4},{6,5},{7,6},{9,8},{10,9},{11,10},{12... | collective-permute-start | bytes 393224 | tf_op jit(solution)/shard_map/ppermute | solution.py:40
  8.5 4.3 %collective-permute-start.3 = (f32[256,128]{1,0:T(8,128)S(1)}, f32[256,128]{1,0:T(8,128)S(1)}, u32[]{:S(2)}, u32[]{:S(2)}) collective-permute-start(f32[256,128]{1,0:T(8,128)S(1)} %get-tuple-element.26), channel_id=1, source_target_pairs={{0,1},{1,2},{2,3},{3,4},{4,5},{5,6},{6,7},{8,9},{9,10},{10,11},{11... | collective-permute-start | bytes 393224 | tf_op jit(solution)/shard_map/ppermute | solution.py:40
  12.8 0.1 collective-permute-start.4
  12.8 0.5 collective-permute-start.5
  13.3 0.1 copy.18
  13.4 2.5 %collective-permute-start = (s32[48,2]{1,0:T(8,128)S(1)}, s32[48,2]{1,0:T(8,128)S(1)}, u32[]{:S(2)}, u32[]{:S(2)}) collective-permute-start(s32[48,2]{1,0:T(8,128)S(1)} %copy.18), channel_id=1, source_target_pairs={{0,1},{1,2},{2,3},{3,4},{4,5},{5,6},{6,7},{8,9},{9,10},{10,11},{11... | collective-permute-start | bytes 1160 | tf_op jit(solution)/shard_map/ppermute | solution.py:40
  16.6 0.1 copy.19
  16.7 0.6 copy-done.14
  17.3 0.1 copy.20
  17.4 1.7 %collective-permute-done.behind_depth = s32[48,2]{1,0:T(8,128)S(1)} collective-permute-done((s32[48,2]{1,0:T(8,128)S(1)}, s32[48,2]{1,0:T(8,128)S(1)}, u32[]{:S(2)}, u32[]{:S(2)}) %collective-permute-start) | collective-permute-done | bytes 416 | tf_op jit(solution)/shard_map/ppermute | solution.py:40
  19.1 28.8 %local_tiles.2 = (f32[32,32,128]{2,1,0:T(8,128)S(1)}, bf16[32,128,32]{2,1,0:T(8,128)(2,1)S(1)}) custom-call(s32[128,2]{1,0:T(8,128)S(1)} %bitcast.33, s32[1,1]{1,0:T(1,128)S(6)} %copy.21.total, f32[16,32,128]{2,1,0:T(8,128)S(1)} %get-tuple-element.22.state), custom_call_target="tpu_custom_call" | custom-call | flops 1258291200 | bytes 8388608 | tf_op jit(solution)/shard_map/local_tiles/pallas_call | solution.py:408
  48.0 0.0 copy-start.6
  48.0 0.0 copy-start.7
  48.0 0.1 copy.17
  48.2 0.5 copy-done.6
  48.7 0.0 copy-done.7
  48.8 0.1 copy-done.11
  48.9 28.5 %half_step.1 = (f32[16,32,128]{2,1,0:T(8,128)S(1)}, f32[256,128]{1,0:T(8,128)S(1)}, f32[256,128]{1,0:T(8,128)S(1)}, f32[256,128]{1,0:T(8,128)S(1)}, f32[256,128]{1,0:T(8,128)S(1)}) custom-call(s32[4,16]{1,0:T(4,128)S(1)} %bitcast.36, s32[2,48,2]{2,1,0:T(8,128)S(1)} %bitcast.23, s32[48,2]{1,0:T(8,128)S(1)} %collective-permute-done.behind_depth, ...), custom_call_target="tpu_custom_call" | custom-call | tf_op jit(solution)/shard_map/half_step/pallas_call | solution.py:436
  77.4 1.9 %collective-permute-start.6 = (f32[256,128]{1,0:T(8,128)S(1)}, f32[256,128]{1,0:T(8,128)S(1)}, u32[]{:S(2)}, u32[]{:S(2)}) collective-permute-start(f32[256,128]{1,0:T(8,128)S(1)} %get-tuple-element.32), channel_id=1, source_target_pairs={{1,0},{2,1},{3,2},{4,3},{5,4},{6,5},{7,6},{9,8},{10,9},{11,10},{12... | collective-permute-start | bytes 393224 | tf_op jit(solution)/shard_map/ppermute | solution.py:40
  79.3 4.8 %collective-permute-start.7 = (f32[256,128]{1,0:T(8,128)S(1)}, f32[256,128]{1,0:T(8,128)S(1)}, u32[]{:S(2)}, u32[]{:S(2)}) collective-permute-start(f32[256,128]{1,0:T(8,128)S(1)} %get-tuple-element.33), channel_id=1, source_target_pairs={{0,1},{1,2},{2,3},{3,4},{4,5},{5,6},{6,7},{8,9},{9,10},{10,11},{11... | collective-permute-start | bytes 393224 | tf_op jit(solution)/shard_map/ppermute | solution.py:40
  84.1 0.1 collective-permute-start.8
  84.2 0.5 collective-permute-start.9
  84.7 28.9 %local_tiles.3 = (f32[32,32,128]{2,1,0:T(8,128)S(1)}, bf16[32,128,32]{2,1,0:T(8,128)(2,1)S(1)}) custom-call(s32[128,2]{1,0:T(8,128)S(1)} %bitcast.34, s32[1,1]{1,0:T(1,128)S(6)} %copy.21.total, f32[16,32,128]{2,1,0:T(8,128)S(1)} %get-tuple-element.29.state), custom_call_target="tpu_custom_call" | custom-call | flops 1258291200 | bytes 8388608 | tf_op jit(solution)/shard_map/local_tiles/pallas_call | solution.py:408
  113.6 0.0 collective-permute-done.6.d_next
  113.7 29.2 %full_step.1 = (f32[3,32,128]{2,1,0:T(8,128)}, f32[3,32,128]{2,1,0:T(8,128)}, f32[6,32,128]{2,1,0:T(8,128)}, f32[32,128]{1,0:T(8,128)}) custom-call(s32[4,16]{1,0:T(4,128)S(1)} %bitcast.37, s32[2,48,2]{2,1,0:T(8,128)S(1)} %bitcast.24, s32[48,2]{1,0:T(8,128)S(1)} %collective-permute-done.behind_depth, s32[48,2]{1,0:T(8,128)S(1)} %collective-permute-done.1.behind_strip, ...), custom_call_target="tpu_custom_call" | custom-call | tf_op jit(solution)/shard_map/full_step/pallas_call | solution.py:450
  (28 shorter events, 0.1 us)
Async XLA Ops:
  0.6 0.7 copy-start.8
  0.6 0.7 copy-start.12
  1.3 0.9 copy-start
  2.2 0.8 copy-start.2
  3.0 0.8 copy-start.4
  3.8 0.7 copy-start.9
  4.5 0.7 copy-start.10
  6.0 42.2 %collective-permute-start.2 = (f32[256,128]{1,0:T(8,128)S(1)}, f32[256,128]{1,0:T(8,128)S(1)}, u32[]{:S(2)}, u32[]{:S(2)}) collective-permute-start(f32[256,128]{1,0:T(8,128)S(1)} %get-tuple-element.25), channel_id=1, source_target_pairs={{1,0},{2,1},{3,2},{4,3},{5,4},{6,5},{7,6},{9,8},{10,9},{11,10},{12... | collective-permute-start | bytes 393224 | tf_op jit(solution)/shard_map/ppermute | solution.py:40
  8.4 4.9 %copy-start.13 = (s32[1,1,2,48,2]{3,4,2,1,0:T(2,128)S(1)}, s32[1,1,2,48,2]{3,4,2,1,0:T(2,128)}, u32[]{:S(2)}) copy-start(s32[1,1,2,48,2]{3,4,2,1,0:T(2,128)} %param.24) | copy-start | bytes 2308
  8.5 39.7 %collective-permute-start.3 = (f32[256,128]{1,0:T(8,128)S(1)}, f32[256,128]{1,0:T(8,128)S(1)}, u32[]{:S(2)}, u32[]{:S(2)}) collective-permute-start(f32[256,128]{1,0:T(8,128)S(1)} %get-tuple-element.26), channel_id=1, source_target_pairs={{0,1},{1,2},{2,3},{3,4},{4,5},{5,6},{6,7},{8,9},{9,10},{10,11},{11... | collective-permute-start | bytes 393224 | tf_op jit(solution)/shard_map/ppermute | solution.py:40
  12.8 35.4 %collective-permute-start.4 = (f32[256,128]{1,0:T(8,128)S(1)}, f32[256,128]{1,0:T(8,128)S(1)}, u32[]{:S(2)}, u32[]{:S(2)}) collective-permute-start(f32[256,128]{1,0:T(8,128)S(1)} %get-tuple-element.27), channel_id=1, source_target_pairs={{0,24},{8,0},{16,8},{24,16},{1,25},{9,1},{17,9},{25,17},{2,26},{10... | collective-permute-start | bytes 393224 | tf_op jit(solution)/shard_map/ppermute | solution.py:46
  12.8 35.4 %collective-permute-start.5 = (f32[256,128]{1,0:T(8,128)S(1)}, f32[256,128]{1,0:T(8,128)S(1)}, u32[]{:S(2)}, u32[]{:S(2)}) collective-permute-start(f32[256,128]{1,0:T(8,128)S(1)} %get-tuple-element.28), channel_id=1, source_target_pairs={{0,8},{8,16},{16,24},{24,0},{1,9},{9,17},{17,25},{25,1},{2,10},{10... | collective-permute-start | bytes 393224 | tf_op jit(solution)/shard_map/ppermute | solution.py:46
  13.4 5.7 %collective-permute-start = (s32[48,2]{1,0:T(8,128)S(1)}, s32[48,2]{1,0:T(8,128)S(1)}, u32[]{:S(2)}, u32[]{:S(2)}) collective-permute-start(s32[48,2]{1,0:T(8,128)S(1)} %copy.18), channel_id=1, source_target_pairs={{0,1},{1,2},{2,3},{3,4},{4,5},{5,6},{6,7},{8,9},{9,10},{10,11},{11... | collective-permute-start | bytes 1160 | tf_op jit(solution)/shard_map/ppermute | solution.py:40
  16.6 0.7 copy-start.14
  19.1 29.0 %collective-permute-start.1 = (s32[48,2]{1,0:T(8,128)S(1)}, s32[48,2]{1,0:T(8,128)S(1)}, u32[]{:S(2)}, u32[]{:S(2)}) collective-permute-start(s32[48,2]{1,0:T(8,128)S(1)} %copy.19), channel_id=1, source_target_pairs={{0,8},{8,16},{16,24},{24,0},{1,9},{9,17},{17,25},{25,1},{2,10},{10... | collective-permute-start | bytes 1160 | tf_op jit(solution)/shard_map/ppermute | solution.py:46
  19.1 29.1 %copy-start.1 = (f32[1,1,6,32,128]{4,3,2,1,0:T(8,128)S(1)}, f32[1,1,6,32,128]{4,3,2,1,0:T(8,128)}, u32[]{:S(2)}) copy-start(f32[1,1,6,32,128]{4,3,2,1,0:T(8,128)} %param.15) | copy-start | bytes 294916
  48.0 0.8 copy-start.6
  48.0 0.7 copy-start.7
  48.2 0.7 copy-start.11
  77.4 36.3 %collective-permute-start.6 = (f32[256,128]{1,0:T(8,128)S(1)}, f32[256,128]{1,0:T(8,128)S(1)}, u32[]{:S(2)}, u32[]{:S(2)}) collective-permute-start(f32[256,128]{1,0:T(8,128)S(1)} %get-tuple-element.32), channel_id=1, source_target_pairs={{1,0},{2,1},{3,2},{4,3},{5,4},{6,5},{7,6},{9,8},{10,9},{11,10},{12... | collective-permute-start | bytes 393224 | tf_op jit(solution)/shard_map/ppermute | solution.py:40
  79.3 34.3 %collective-permute-start.7 = (f32[256,128]{1,0:T(8,128)S(1)}, f32[256,128]{1,0:T(8,128)S(1)}, u32[]{:S(2)}, u32[]{:S(2)}) collective-permute-start(f32[256,128]{1,0:T(8,128)S(1)} %get-tuple-element.33), channel_id=1, source_target_pairs={{0,1},{1,2},{2,3},{3,4},{4,5},{5,6},{6,7},{8,9},{9,10},{10,11},{11... | collective-permute-start | bytes 393224 | tf_op jit(solution)/shard_map/ppermute | solution.py:40
  84.1 29.5 %collective-permute-start.8 = (f32[256,128]{1,0:T(8,128)S(1)}, f32[256,128]{1,0:T(8,128)S(1)}, u32[]{:S(2)}, u32[]{:S(2)}) collective-permute-start(f32[256,128]{1,0:T(8,128)S(1)} %get-tuple-element.34), channel_id=1, source_target_pairs={{0,24},{8,0},{16,8},{24,16},{1,25},{9,1},{17,9},{25,17},{2,26},{10... | collective-permute-start | bytes 393224 | tf_op jit(solution)/shard_map/ppermute | solution.py:46
  84.2 29.5 %collective-permute-start.9 = (f32[256,128]{1,0:T(8,128)S(1)}, f32[256,128]{1,0:T(8,128)S(1)}, u32[]{:S(2)}, u32[]{:S(2)}) collective-permute-start(f32[256,128]{1,0:T(8,128)S(1)} %get-tuple-element.35), channel_id=1, source_target_pairs={{0,8},{8,16},{16,24},{24,0},{1,9},{9,17},{17,25},{25,1},{2,10},{10... | collective-permute-start | bytes 393224 | tf_op jit(solution)/shard_map/ppermute | solution.py:46
  84.7 29.0 %copy-start.3 = (f32[1,1,3,32,128]{4,3,2,1,0:T(8,128)S(1)}, f32[1,1,3,32,128]{4,3,2,1,0:T(8,128)}, u32[]{:S(2)}) copy-start(f32[1,1,3,32,128]{4,3,2,1,0:T(8,128)} %param.13) | copy-start | bytes 147460
  84.7 29.0 %copy-start.5 = (f32[1,1,3,32,128]{4,3,2,1,0:T(8,128)S(1)}, f32[1,1,3,32,128]{4,3,2,1,0:T(8,128)}, u32[]{:S(2)}) copy-start(f32[1,1,3,32,128]{4,3,2,1,0:T(8,128)} %param.14) | copy-start | bytes 147460
